TPU v7x, 1024 devices: a whole 8x8x8 slice. The times are simulated.
1024 devices in a mesh: lon: 64 (over y_lo, x, core), lat: 16 (over y_hi, z).
Axes of the slice: x: 8, y: 8 (y_hi: 2, y_lo: 4; y = y_hi * 4 + y_lo), z: 8, core: 2. Of those that a mesh axis runs over, the one named last changes fastest.
Arguments:
- record_values: bfloat16 [4096, 256, 2, 128], P('lon', 'lat'), may hold values from -6 to 6
- record_cell: int32 [4096, 256, 2], P('lon', 'lat'), may hold values from 0 to 287
- record_instrument: int32 [4096, 256, 2], P('lon', 'lat'), may hold values from 0 to 7
- block_counts: int32 [4096, 256], P('lon', 'lat'), may hold values from 0 to 2, as said below
- background: bfloat16 [192, 1536, 2, 192], P('lat', 'lon'), may hold values from -6 to 6
- input_weight: bfloat16 [128, 192], replicated, may hold values from -0.5 to 0.5
- instrument_table: bfloat16 [8, 192], replicated, may hold values from -4 to 4
- lift_weight: bfloat16 [192, 384], replicated, may hold values from -0.4375 to 0.4375
- first_gain: bfloat16 [192], replicated, may hold values from 0.5 to 1.5
- attn_weight: bfloat16 [192, 576], replicated
- mix_weight: bfloat16 [192, 192], replicated, may hold values from -0.4375 to 0.4375
- second_gain: bfloat16 [192], replicated, may hold values from 0.5 to 1.5
- up_weight: bfloat16 [192, 768], replicated, may hold values from -0.4375 to 0.4375
- down_weight: bfloat16 [768, 192], replicated, may hold values from -0.21875 to 0.21875
Outputs:
- result: bfloat16 [192, 1536, 2, 192], P('lat', 'lon')
Inputs may be any that keep to these rules, and one draw needn't show every extreme that they name: `block_counts`: each block's count is at most 2; for some tiles every source fills all 2 slots.
All inputs are finite; a program needn't handle non-finite values.
Results may differ from a plain program's by a relative error of at most 0.017.
Values may be sent and summed in bfloat16 or wider, within the bound.
A program may use at most 32 MiB of HBM per device.

v0:
```python
import jax
import jax.numpy as jnp
from jax import lax
from jax.sharding import PartitionSpec as P

HEADS = 6
INSTR = 8
LEV = 2
WLAT = 6
WLON = 12


def shifted(value, axis, steps):
    count = lax.axis_size(axis)
    pairs = [(source, (source + steps) % count) for source in range(count)]
    return lax.ppermute(value, axis, pairs)


def layer_norm(tensor, norm_gain):
    wide = tensor.astype(jnp.float32)
    average = jnp.mean(wide, axis=-1, keepdims=True)
    centred = wide - average
    spread = jnp.mean(centred * centred, axis=-1, keepdims=True)
    return (centred * lax.rsqrt(spread + 1e-05) * norm_gain.astype(jnp.float32)).astype(
        jnp.bfloat16
    )


def to_windows(tensor):
    height, breadth, levels, width = tensor.shape
    shaped = tensor.reshape(height // WLAT, WLAT, breadth // WLON, WLON, levels, width)
    shaped = shaped.transpose(0, 2, 1, 3, 4, 5)
    return shaped.reshape(height // WLAT * (breadth // WLON), WLAT * WLON * levels, width)


def from_windows(tensor, height, breadth):
    width = tensor.shape[-1]
    shaped = tensor.reshape(height // WLAT, breadth // WLON, WLAT, WLON, LEV, width)
    return shaped.transpose(0, 2, 1, 3, 4, 5).reshape(height, breadth, LEV, width)


def encode_records(values, instrument_tag, input_weight, instrument_table):
    flat = values.reshape(-1, values.shape[-1])
    tags = instrument_tag.reshape(-1)
    chooser = (tags[:, None] == jnp.arange(INSTR, dtype=jnp.float32)[None, :]).astype(jnp.bfloat16)
    before = jnp.dot(flat, input_weight, preferred_element_type=jnp.float32)
    before = before + jnp.dot(chooser, instrument_table, preferred_element_type=jnp.float32)
    encoded = jax.nn.gelu(before).astype(jnp.bfloat16)
    return encoded.reshape(values.shape[:-1] + (input_weight.shape[1],))


def attend_windows(tokens, rows_global, grid_rows, attn_weight):
    height, breadth, levels, width = tokens.shape
    head_size = width // HEADS
    projected = jnp.dot(tokens.reshape(-1, width), attn_weight, preferred_element_type=jnp.float32)
    projected = projected.reshape(height, breadth, levels, 3 * width)
    query = (projected[..., :width] * head_size ** (-0.5)).astype(jnp.bfloat16)
    keys = projected[..., width : 2 * width].astype(jnp.bfloat16)
    value_rows = projected[..., 2 * width :].astype(jnp.bfloat16)
    region = (rows_global >= grid_rows - WLAT // 2).astype(jnp.float32)
    region = jnp.broadcast_to(region[:, None, None, None], (height, breadth, levels, 1))
    region_w = to_windows(region)[..., 0]
    windows = region_w.shape[0]
    count_tok = region_w.shape[1]
    query_w = to_windows(query).reshape(windows, count_tok, HEADS, head_size)
    keys_w = to_windows(keys).reshape(windows, count_tok, HEADS, head_size)
    values_w = to_windows(value_rows).reshape(windows, count_tok, HEADS, head_size)
    scores = jnp.einsum("wqhd,wkhd->whqk", query_w, keys_w, preferred_element_type=jnp.float32)
    allowed = region_w[:, None, :, None] == region_w[:, None, None, :]
    scores = jnp.where(allowed, scores, jnp.float32(-1e30))
    largest = jnp.max(scores, axis=-1, keepdims=True)
    raised = jnp.exp(scores - largest)
    attn_weights = (raised / jnp.sum(raised, axis=-1, keepdims=True)).astype(jnp.bfloat16)
    output = jnp.einsum(
        "whqk,wkhd->wqhd", attn_weights, values_w, preferred_element_type=jnp.float32
    )
    output = output.astype(jnp.bfloat16).reshape(windows, count_tok, width)
    return from_windows(output, height, breadth)


def local(
    record_values,
    record_cell,
    record_instrument,
    block_counts,
    background,
    input_weight,
    instrument_table,
    lift_weight,
    first_gain,
    attn_weight,
    mix_weight,
    second_gain,
    up_weight,
    down_weight,
):
    lat_cells = background.shape[0]
    lon_cells = background.shape[1]
    width = background.shape[3]
    capacity = record_values.shape[2]
    is_live = jnp.arange(capacity, dtype=jnp.int32)[None, None, :] < block_counts[:, :, None]
    row_index = jnp.where(is_live, record_cell // lon_cells, -1).astype(jnp.bfloat16)
    col_index = (record_cell % lon_cells).astype(jnp.bfloat16)
    encoded = encode_records(
        record_values, record_instrument.astype(jnp.float32), input_weight, instrument_table
    )
    encoded, row_index, col_index = (
        lax.all_to_all(
            lax.all_to_all(encoded, "lon", split_axis=0, concat_axis=0, tiled=True),
            "lat",
            split_axis=1,
            concat_axis=1,
            tiled=True,
        ),
        lax.all_to_all(
            lax.all_to_all(row_index, "lon", split_axis=0, concat_axis=0, tiled=True),
            "lat",
            split_axis=1,
            concat_axis=1,
            tiled=True,
        ),
        lax.all_to_all(
            lax.all_to_all(col_index, "lon", split_axis=0, concat_axis=0, tiled=True),
            "lat",
            split_axis=1,
            concat_axis=1,
            tiled=True,
        ),
    )
    lifted = jnp.dot(encoded.reshape(-1, width), lift_weight, preferred_element_type=jnp.float32)
    lifted = jax.nn.gelu(lifted).astype(jnp.bfloat16)
    row_float = row_index.reshape(-1).astype(jnp.float32)
    col_float = col_index.reshape(-1).astype(jnp.float32)
    cell_value = jnp.where(row_float < 0.0, -1.0, row_float * lon_cells + col_float)
    cell_ids = jnp.arange(lat_cells * lon_cells, dtype=jnp.float32)
    onehot = (cell_ids[:, None] == cell_value[None, :]).astype(jnp.bfloat16)
    summed = jnp.dot(onehot, lifted, preferred_element_type=jnp.float32)
    tallies = jnp.sum(onehot, axis=1, dtype=jnp.float32)
    latent = (background.astype(jnp.float32) + summed.reshape(lat_cells, lon_cells, LEV, width)) / (
        1.0 + tallies
    ).reshape(lat_cells, lon_cells, 1, 1)
    latent = latent.astype(jnp.bfloat16)
    normed = layer_norm(latent, first_gain)
    grid_rows = lat_cells * lax.axis_size("lat")
    lat_start = lax.axis_index("lat") * lat_cells
    half_lat = WLAT // 2
    half_lon = WLON // 2
    ahead = shifted(normed[:, :half_lon], "lon", -1)
    moved = jnp.concatenate([normed[:, half_lon:], ahead], axis=1)
    above = shifted(moved[:half_lat], "lat", -1)
    moved = jnp.concatenate([moved[half_lat:], above], axis=0)
    rows_global = (lat_start + jnp.arange(lat_cells, dtype=jnp.int32) + half_lat) % grid_rows
    mixed_rolled = attend_windows(moved, rows_global, grid_rows, attn_weight)
    below = shifted(mixed_rolled[lat_cells - half_lat :], "lat", 1)
    returned = jnp.concatenate([below, mixed_rolled[: lat_cells - half_lat]], axis=0)
    behind = shifted(returned[:, lon_cells - half_lon :], "lon", 1)
    mixed = jnp.concatenate([behind, returned[:, : lon_cells - half_lon]], axis=1)
    after_attn = latent.astype(jnp.float32) + jnp.dot(
        mixed.reshape(-1, width), mix_weight, preferred_element_type=jnp.float32
    ).reshape(lat_cells, lon_cells, LEV, width)
    after_attn = after_attn.astype(jnp.bfloat16)
    normed_two = layer_norm(after_attn, second_gain)
    hidden = jax.nn.gelu(
        jnp.dot(normed_two.reshape(-1, width), up_weight, preferred_element_type=jnp.float32)
    ).astype(jnp.bfloat16)
    result = after_attn.astype(jnp.float32) + jnp.dot(
        hidden, down_weight, preferred_element_type=jnp.float32
    ).reshape(lat_cells, lon_cells, LEV, width)
    return result.astype(jnp.bfloat16)


def solution(mesh):
    placed = (
        P("lon", "lat", None, None),
        P("lon", "lat", None),
        P("lon", "lat", None),
        P("lon", "lat"),
        P("lat", "lon", None, None),
        P(),
        P(),
        P(),
        P(),
        P(),
        P(),
        P(),
        P(),
        P(),
    )
    return jax.shard_map(
        local, mesh=mesh, in_specs=placed, out_specs=P("lat", "lon", None, None), check_vma=False
    )
```

profile of v0, /device:TPU:32, one launch (start us, length us, event | category | flops | bytes accessed | tf_op | source)
XLA Modules:
  0.0 212.4 jit_solution(16865898530616870388)
XLA Ops:
  0.0 0.9 copy.110
  0.9 0.8 copy.109
  1.7 0.9 fusion.69
  2.6 17.0 %all-to-all-start = ((bf16[64,16,2]{1,2,0:T(2,128)(2,1)}), bf16[64,16,2]{1,2,0:T(2,128)(2,1)S(1)}, u32[]{:S(2)}, u32[]{:S(2)}) async-start(bf16[64,16,2]{1,2,0:T(2,128)(2,1)} %get-tuple-element.10), calls=%async_computation | async-start | bytes 65536 | tf_op jit(solution)/shard_map/all_to_all | solution.py:116
  19.6 0.7 convert_element_type.99
  20.9 6.7 %all-to-all-done = bf16[64,16,2]{1,2,0:T(2,128)(2,1)S(1)} async-done(((bf16[64,16,2]{1,2,0:T(2,128)(2,1)}), bf16[64,16,2]{1,2,0:T(2,128)(2,1)S(1)}, u32[]{:S(2)}, u32[]{:S(2)}) %all-to-all-start) | async-done | bytes 4128 | tf_op jit(solution)/shard_map/all_to_all | solution.py:116
  27.6 6.4 %all-to-all-start.2 = ((bf16[64,16,2]{1,2,0:T(2,128)(2,1)}), bf16[64,16,2]{1,2,0:T(2,128)(2,1)S(1)}, u32[]{:S(2)}, u32[]{:S(2)}) async-start(bf16[64,16,2]{1,2,0:T(2,128)(2,1)} %get-tuple-element.9), calls=%async_computation.2 | async-start | bytes 65536 | tf_op jit(solution)/shard_map/all_to_all | solution.py:123
  34.0 1.3 fusion.39
  35.3 0.7 copy.113
  36.0 5.9 %all-to-all-done.2 = bf16[64,16,2]{1,2,0:T(2,128)(2,1)S(1)} async-done(((bf16[64,16,2]{1,2,0:T(2,128)(2,1)}), bf16[64,16,2]{1,2,0:T(2,128)(2,1)S(1)}, u32[]{:S(2)}, u32[]{:S(2)}) %all-to-all-start.2) | async-done | bytes 4128 | tf_op jit(solution)/shard_map/all_to_all | solution.py:123
  41.9 13.7 %all-to-all-start.1 = ((bf16[64,16,2]{0,2,1:T(2,128)(2,1)}), bf16[64,16,2]{0,2,1:T(2,128)(2,1)S(1)}, u32[]{:S(2)}, u32[]{:S(2)}) async-start(bf16[64,16,2]{0,2,1:T(2,128)(2,1)} %copy.113), calls=%async_computation.1 | async-start | bytes 16384 | tf_op jit(solution)/shard_map/all_to_all | solution.py:115
  55.7 0.7 fusion.32
  56.4 0.5 copy.117
  56.9 1.4 reshape.129
  58.2 9.6 %all-to-all-done.1 = bf16[64,16,2]{0,2,1:T(2,128)(2,1)S(1)} async-done(((bf16[64,16,2]{0,2,1:T(2,128)(2,1)}), bf16[64,16,2]{0,2,1:T(2,128)(2,1)S(1)}, u32[]{:S(2)}, u32[]{:S(2)}) %all-to-all-start.1) | async-done | bytes 4128 | tf_op jit(solution)/shard_map/all_to_all | solution.py:115
  67.8 6.5 %all-to-all-start.4 = ((bf16[64,16,2,192]{3,2,1,0:T(2,128)(2,1)}), bf16[64,16,2,192]{3,2,1,0:T(2,128)(2,1)S(1)}, u32[]{:S(2)}, u32[]{:S(2)}) async-start(bf16[64,16,2,192]{3,2,1,0:T(2,128)(2,1)} %reshape.129), calls=%async_computation.4 | async-start | bytes 2097152 | tf_op jit(solution)/shard_map/all_to_all | solution.py:109
  74.3 0.7 copy.114
  75.0 26.0 %all-to-all-done.4 = bf16[64,16,2,192]{3,2,1,0:T(2,128)(2,1)S(1)} async-done(((bf16[64,16,2,192]{3,2,1,0:T(2,128)(2,1)}), bf16[64,16,2,192]{3,2,1,0:T(2,128)(2,1)S(1)}, u32[]{:S(2)}, u32[]{:S(2)}) %all-to-all-start.4) | async-done | bytes 786464 | tf_op jit(solution)/shard_map/all_to_all | solution.py:109
  101.0 3.5 %all-to-all-start.3 = ((bf16[64,16,2]{0,2,1:T(2,128)(2,1)}), bf16[64,16,2]{0,2,1:T(2,128)(2,1)S(1)}, u32[]{:S(2)}, u32[]{:S(2)}) async-start(bf16[64,16,2]{0,2,1:T(2,128)(2,1)} %copy.114), calls=%async_computation.3 | async-start | bytes 16384 | tf_op jit(solution)/shard_map/all_to_all | solution.py:122
  104.5 2.0 copy.118
  106.5 10.2 %all-to-all-done.3 = bf16[64,16,2]{0,2,1:T(2,128)(2,1)S(1)} async-done(((bf16[64,16,2]{0,2,1:T(2,128)(2,1)}), bf16[64,16,2]{0,2,1:T(2,128)(2,1)S(1)}, u32[]{:S(2)}, u32[]{:S(2)}) %all-to-all-start.3) | async-done | bytes 4128 | tf_op jit(solution)/shard_map/all_to_all | solution.py:122
  116.7 3.8 %all-to-all-start.5 = ((bf16[64,16,2,192]{3,2,0,1:T(2,128)(2,1)}), bf16[64,16,2,192]{3,2,0,1:T(2,128)(2,1)S(1)}, u32[]{:S(2)}, u32[]{:S(2)}) async-start(bf16[64,16,2,192]{3,2,0,1:T(2,128)(2,1)} %copy.118), calls=%async_computation.5 | async-start | bytes 2097152 | tf_op jit(solution)/shard_map/all_to_all | solution.py:108
  121.9 33.4 %all-to-all-done.5 = bf16[64,16,2,192]{3,2,0,1:T(2,128)(2,1)S(1)} async-done(((bf16[64,16,2,192]{3,2,0,1:T(2,128)(2,1)}), bf16[64,16,2,192]{3,2,0,1:T(2,128)(2,1)S(1)}, u32[]{:S(2)}, u32[]{:S(2)}) %all-to-all-start.5) | async-done | bytes 786464 | tf_op jit(solution)/shard_map/all_to_all | solution.py:108
  155.3 1.1 copy.119
  156.5 1.0 reshape.130
  157.5 1.7 fusion.13
  160.6 1.9 collective-permute-start
  162.5 0.8 broadcast_compare_fusion
  163.4 1.3 collective-permute-done
  164.7 6.8 %collective-permute-start.1 = (bf16[3,24,2,192]{3,1,2,0:T(8,128)(2,1)S(1)}, bf16[3,24,2,192]{3,1,2,0:T(8,128)(2,1)S(1)}, u32[]{:S(2)}, u32[]{:S(2)}) collective-permute-start(bf16[3,24,2,192]{3,1,2,0:T(8,128)(2,1)S(1)} %pad_maximum_fusion), channel_id=1, source_target_pairs={{0,15},{1,0},{2,1},{3,2},{4,3},{5,4},{6,5},{7,6},{8,7},{9,8},{10,9... | collective-permute-start | bytes 165896 | tf_op jit(solution)/shard_map/ppermute | solution.py:16
  171.6 2.1 %collective-permute-done.1 = bf16[3,24,2,192]{3,1,2,0:T(8,128)(2,1)S(1)} collective-permute-done((bf16[3,24,2,192]{3,1,2,0:T(8,128)(2,1)S(1)}, bf16[3,24,2,192]{3,1,2,0:T(8,128)(2,1)S(1)}, u32[]{:S(2)}, u32[]{:S(2)}) %collective-permute-start.1) | collective-permute-done | bytes 55328 | tf_op jit(solution)/shard_map/ppermute | solution.py:16
  174.2 0.8 fusion.83
  175.2 0.9 copy.126
  176.2 1.9 reshape_reshape.14
  178.4 0.9 copy.124
  179.3 1.9 reshape_reshape.13
  181.7 1.6 reshape_reshape.12
  183.3 0.6 fusion.41
  184.2 1.2 fusion.85
  185.5 0.5 fusion.37
  186.0 0.6 copy.131
  186.6 0.7 reshape_reshape.15
  187.6 1.9 collective-permute-start.2
  189.7 10.9 %collective-permute-done.2 = bf16[3,24,2,192]{3,1,2,0:T(8,128)(2,1)S(1)} collective-permute-done((bf16[3,24,2,192]{3,1,2,0:T(8,128)(2,1)S(1)}, bf16[3,24,2,192]{3,1,2,0:T(8,128)(2,1)S(1)}, u32[]{:S(2)}, u32[]{:S(2)}) %collective-permute-start.2) | collective-permute-done | bytes 55328 | tf_op jit(solution)/shard_map/ppermute | solution.py:16
  200.6 1.9 collective-permute-start.3
  202.6 6.1 %collective-permute-done.3 = bf16[12,6,2,192]{3,1,2,0:T(8,128)(2,1)S(1)} collective-permute-done((bf16[12,6,2,192]{3,1,2,0:T(8,128)(2,1)S(1)}, bf16[12,6,2,192]{3,1,2,0:T(8,128)(2,1)S(1)}, u32[]{:S(2)}, u32[]{:S(2)}) %collective-permute-start.3) | collective-permute-done | bytes 55328 | tf_op jit(solution)/shard_map/ppermute | solution.py:16
  210.2 0.9 fusion.33
  211.5 0.9 copy.138
  (71 shorter events, 7.4 us)
Async XLA Ops:
  0.0 55.6 %copy-start = (bf16[64,16,2,128]{3,2,1,0:T(2,128)(2,1)S(1)}, bf16[64,16,2,128]{3,2,1,0:T(2,128)(2,1)}, u32[]{:S(2)}) copy-start(bf16[64,16,2,128]{3,2,1,0:T(2,128)(2,1)} %param.14) | copy-start | bytes 1572868
  0.0 55.6 %copy-start.10 = (bf16[128,192]{0,1:T(8,128)(2,1)S(1)}, bf16[128,192]{0,1:T(8,128)(2,1)}, u32[]{:S(2)}) copy-start(bf16[128,192]{0,1:T(8,128)(2,1)} %param.19) | copy-start | bytes 147460
  2.6 25.0 %all-to-all-start = ((bf16[64,16,2]{1,2,0:T(2,128)(2,1)}), bf16[64,16,2]{1,2,0:T(2,128)(2,1)S(1)}, u32[]{:S(2)}, u32[]{:S(2)}) async-start(bf16[64,16,2]{1,2,0:T(2,128)(2,1)} %get-tuple-element.10), calls=%async_computation | async-start | bytes 65536 | tf_op jit(solution)/shard_map/all_to_all | solution.py:116
  27.6 14.3 %all-to-all-start.2 = ((bf16[64,16,2]{1,2,0:T(2,128)(2,1)}), bf16[64,16,2]{1,2,0:T(2,128)(2,1)S(1)}, u32[]{:S(2)}, u32[]{:S(2)}) async-start(bf16[64,16,2]{1,2,0:T(2,128)(2,1)} %get-tuple-element.9), calls=%async_computation.2 | async-start | bytes 65536 | tf_op jit(solution)/shard_map/all_to_all | solution.py:123
  41.9 26.0 %all-to-all-start.1 = ((bf16[64,16,2]{0,2,1:T(2,128)(2,1)}), bf16[64,16,2]{0,2,1:T(2,128)(2,1)S(1)}, u32[]{:S(2)}, u32[]{:S(2)}) async-start(bf16[64,16,2]{0,2,1:T(2,128)(2,1)} %copy.113), calls=%async_computation.1 | async-start | bytes 16384 | tf_op jit(solution)/shard_map/all_to_all | solution.py:115
  67.8 33.1 %all-to-all-start.4 = ((bf16[64,16,2,192]{3,2,1,0:T(2,128)(2,1)}), bf16[64,16,2,192]{3,2,1,0:T(2,128)(2,1)S(1)}, u32[]{:S(2)}, u32[]{:S(2)}) async-start(bf16[64,16,2,192]{3,2,1,0:T(2,128)(2,1)} %reshape.129), calls=%async_computation.4 | async-start | bytes 2097152 | tf_op jit(solution)/shard_map/all_to_all | solution.py:109
  101.0 15.7 %all-to-all-start.3 = ((bf16[64,16,2]{0,2,1:T(2,128)(2,1)}), bf16[64,16,2]{0,2,1:T(2,128)(2,1)S(1)}, u32[]{:S(2)}, u32[]{:S(2)}) async-start(bf16[64,16,2]{0,2,1:T(2,128)(2,1)} %copy.114), calls=%async_computation.3 | async-start | bytes 16384 | tf_op jit(solution)/shard_map/all_to_all | solution.py:122
  104.5 16.1 %copy-start.11 = (bf16[192]{0:T(256)(128)(2,1)S(1)}, bf16[192]{0:T(256)(128)(2,1)}, u32[]{:S(2)}) copy-start(bf16[192]{0:T(256)(128)(2,1)} %param.22) | copy-start | bytes 1156
  116.7 38.6 %all-to-all-start.5 = ((bf16[64,16,2,192]{3,2,0,1:T(2,128)(2,1)}), bf16[64,16,2,192]{3,2,0,1:T(2,128)(2,1)S(1)}, u32[]{:S(2)}, u32[]{:S(2)}) async-start(bf16[64,16,2,192]{3,2,0,1:T(2,128)(2,1)} %copy.118), calls=%async_computation.5 | async-start | bytes 2097152 | tf_op jit(solution)/shard_map/all_to_all | solution.py:108
  121.9 35.6 %copy-start.9 = (bf16[192,384]{1,0:T(8,128)(2,1)S(1)}, bf16[192,384]{1,0:T(8,128)(2,1)}, u32[]{:S(2)}) copy-start(bf16[192,384]{1,0:T(8,128)(2,1)} %param.21) | copy-start | bytes 442372
  157.5 2.2 %copy-start.4 = (bf16[12,24,2,192]{3,2,1,0:T(2,128)(2,1)S(1)}, bf16[12,24,2,192]{3,2,1,0:T(2,128)(2,1)}, u32[]{:S(2)}) copy-start(bf16[12,24,2,192]{3,2,1,0:T(2,128)(2,1)} %param.18) | copy-start | bytes 663556
  160.0 13.8 %copy-start.5 = (bf16[192,576]{1,0:T(8,128)(2,1)S(1)}, bf16[192,576]{1,0:T(8,128)(2,1)}, u32[]{:S(2)}) copy-start(bf16[192,576]{1,0:T(8,128)(2,1)} %param.23) | copy-start | bytes 663556
  160.6 4.1 %collective-permute-start = (bf16[12,6,2,192]{3,1,2,0:T(8,128)(2,1)S(1)}, bf16[12,6,2,192]{3,1,2,0:T(8,128)(2,1)S(1)}, u32[]{:S(2)}, u32[]{:S(2)}) collective-permute-start(bf16[12,6,2,192]{3,1,2,0:T(8,128)(2,1)S(1)} %slice.47), channel_id=1, source_target_pairs={{0,1008},{16,0},{32,16},{48,32},{64,48},{80,64},{96,80},{112,96},{... | collective-permute-start | bytes 165896 | tf_op jit(solution)/shard_map/ppermute | solution.py:16
  164.7 9.0 %collective-permute-start.1 = (bf16[3,24,2,192]{3,1,2,0:T(8,128)(2,1)S(1)}, bf16[3,24,2,192]{3,1,2,0:T(8,128)(2,1)S(1)}, u32[]{:S(2)}, u32[]{:S(2)}) collective-permute-start(bf16[3,24,2,192]{3,1,2,0:T(8,128)(2,1)S(1)} %pad_maximum_fusion), channel_id=1, source_target_pairs={{0,15},{1,0},{2,1},{3,2},{4,3},{5,4},{6,5},{7,6},{8,7},{9,8},{10,9... | collective-permute-start | bytes 165896 | tf_op jit(solution)/shard_map/ppermute | solution.py:16
  178.1 3.1 %copy-start.2 = (bf16[12,24,2,192]{3,1,2,0:T(8,128)(2,1)S(1)}, bf16[12,24,2,192]{3,1,2,0:T(8,128)(2,1)}, u32[]{:S(2)}) copy-start(bf16[12,24,2,192]{3,1,2,0:T(8,128)(2,1)} %get-tuple-element.7) | copy-start | bytes 663556
  183.3 0.9 copy-start.3
  184.2 1.3 copy-start.1
  186.6 16.0 %copy-start.12 = (bf16[192]{0:T(256)(128)(2,1)S(1)}, bf16[192]{0:T(256)(128)(2,1)}, u32[]{:S(2)}) copy-start(bf16[192]{0:T(256)(128)(2,1)} %param.25) | copy-start | bytes 1156
  186.6 22.1 %copy-start.6 = (bf16[192,192]{1,0:T(8,128)(2,1)S(1)}, bf16[192,192]{1,0:T(8,128)(2,1)}, u32[]{:S(2)}) copy-start(bf16[192,192]{1,0:T(8,128)(2,1)} %param.24) | copy-start | bytes 221188
  187.6 12.9 %collective-permute-start.2 = (bf16[3,24,2,192]{3,1,2,0:T(8,128)(2,1)S(1)}, bf16[3,24,2,192]{3,1,2,0:T(8,128)(2,1)S(1)}, u32[]{:S(2)}, u32[]{:S(2)}) collective-permute-start(bf16[3,24,2,192]{3,1,2,0:T(8,128)(2,1)S(1)} %copy.143), channel_id=1, source_target_pairs={{0,1},{1,2},{2,3},{3,4},{4,5},{5,6},{6,7},{7,8},{8,9},{9,10},{10,1... | collective-permute-start | bytes 165896 | tf_op jit(solution)/shard_map/ppermute | solution.py:16
  200.6 8.0 %collective-permute-start.3 = (bf16[12,6,2,192]{3,1,2,0:T(8,128)(2,1)S(1)}, bf16[12,6,2,192]{3,1,2,0:T(8,128)(2,1)S(1)}, u32[]{:S(2)}, u32[]{:S(2)}) collective-permute-start(bf16[12,6,2,192]{3,1,2,0:T(8,128)(2,1)S(1)} %slice.55), channel_id=1, source_target_pairs={{0,16},{16,32},{32,48},{48,64},{64,80},{80,96},{96,112},{112,128},... | collective-permute-start | bytes 165896 | tf_op jit(solution)/shard_map/ppermute | solution.py:16
  208.7 1.5 copy-start.7
  208.7 1.5 copy-start.8
where the time goes:
time: 213 us; the launch traced here: 212 us
  waiting for transfers between devices  112 us (53%)
  starting transfers between devices  63.5 us (30%)
  local copies, waits for them, and re-layouts  24 us (11%)
  matrix products  6.51 us (3%)
  other arithmetic  5.71 us (3%)
    all_to_all x1, waiting for transfers between devices, local(): lax.all_to_all(lax.all_to_all(encoded, 'lon', split_axis=0, concat_axis=0...  33.4 us
    all_to_all x1, waiting for transfers between devices, local(): lax.all_to_all(encoded, 'lon', split_axis=0, concat_axis=0, tiled=True)  26 us
    ppermute x4, waiting for transfers between devices, shifted(): return lax.ppermute(value, axis, pairs)  20.4 us
    all_to_all x1, starting transfers between devices, local(): lax.all_to_all(row_index, 'lon', split_axis=0, concat_axis=0, tiled=True)  17 us
    all_to_all x1, starting transfers between devices, local(): lax.all_to_all(lax.all_to_all(row_index, 'lon', split_axis=0, concat_axis...  13.7 us
    ppermute x4, starting transfers between devices, shifted(): return lax.ppermute(value, axis, pairs)  12.6 us
    all_to_all x1, waiting for transfers between devices, local(): lax.all_to_all(lax.all_to_all(col_index, 'lon', split_axis=0, concat_axis...  10.2 us
    all_to_all x1, waiting for transfers between devices, local(): lax.all_to_all(lax.all_to_all(row_index, 'lon', split_axis=0, concat_axis...  9.6 us
  transfers between devices with their start and end apart: 10, of which 10 were waited for; matrix products, arithmetic and copies ran while one was open for 5% of the time, Pallas kernels for 0%

commit v1 on v0

v1 whole, which is shorter than its diff:
```python
import functools

import jax
import jax.numpy as jnp
import numpy as np
from jax import lax
from jax.experimental import pallas as pl
from jax.experimental.pallas import tpu as pltpu
from jax.sharding import PartitionSpec as P

MESH = pl.DeviceIdType.MESH
HEADS = 6
INSTR = 8
LEV = 2
WLAT = 6
WLON = 12
FAR = -1e30

ROW_CUTS = (0, 3, 9, 12)
COL_CUTS = (0, 6, 18, 24)
ORDER = (("C", 1, 1), ("c00", 0, 0), ("T", 0, 1), ("c03", 0, 2), ("R", 1, 2), ("c33", 2, 2), ("B", 2, 1), ("c30", 2, 0), ("L", 1, 0))


def piece_table():
    table, cells = {}, 0
    for name, i, j in ORDER:
        count = (ROW_CUTS[i + 1] - ROW_CUTS[i]) * (COL_CUTS[j + 1] - COL_CUTS[j])
        padded = -(-count // 8) * 8
        table[name] = (cells, count, padded)
        cells += padded
    return table, cells


PIECES, CELLS = piece_table()
TOKENS = LEV * CELLS
HALO = 896
WIDE = 448


def base_of(i, j):
    name = [n for n, a, b in ORDER if (a, b) == (i, j)][0]
    return PIECES[name][0]


def cell_permutation():
    matrix = np.zeros((CELLS, 288), np.float32)
    for _, i, j in ORDER:
        breadth = COL_CUTS[j + 1] - COL_CUTS[j]
        for r in range(ROW_CUTS[i], ROW_CUTS[i + 1]):
            for c in range(COL_CUTS[j], COL_CUTS[j + 1]):
                place = base_of(i, j) + (r - ROW_CUTS[i]) * breadth + c - COL_CUTS[j]
                matrix[place, r * 24 + c] = 1.0
    return matrix


def dot_nn(a, b):
    return lax.dot_general(a, b, (((1,), (0,)), ((), ())), preferred_element_type=jnp.float32)


def dot_nt(a, b):
    return lax.dot_general(a, b, (((1,), (1,)), ((), ())), preferred_element_type=jnp.float32)


def dot_tn(a, b):
    return lax.dot_general(a, b, (((0,), (0,)), ((), ())), preferred_element_type=jnp.float32)


def norm(wide, gain):
    average = jnp.mean(wide, axis=-1, keepdims=True)
    centred = wide - average
    spread = jnp.mean(centred * centred, axis=-1, keepdims=True)
    return (centred * lax.rsqrt(spread + 1e-05) * gain).astype(jnp.bfloat16)


def gelu(x):
    return jax.nn.gelu(x, approximate=True)


def place_of(cell):
    row = jnp.floor((cell + 0.5) * (1.0 / 24.0))
    col = cell - 24.0 * row
    place = jnp.zeros_like(cell)
    for _, i, j in ORDER:
        breadth = COL_CUTS[j + 1] - COL_CUTS[j]
        inside = (row >= ROW_CUTS[i]) & (row < ROW_CUTS[i + 1]) & (col >= COL_CUTS[j]) & (col < COL_CUTS[j + 1])
        value = base_of(i, j) + (row - ROW_CUTS[i]) * breadth + (col - COL_CUTS[j])
        place = jnp.where(inside, value, place)
    return place


def kernel(
    n_lon,
    n_lat,
    values_hbm,
    cell_ref,
    instr_ref,
    count_ref,
    back_ref,
    perm_ref,
    win_ref,
    table_ref,
    lift_ref,
    gain1_ref,
    attn_ref,
    mix_ref,
    gain2_ref,
    up_ref,
    down_ref,
    out_ref,
    buf1,
    buf2,
    meta_s,
    meta_r,
    meta2_s,
    meta2_r,
    onehot_s,
    lifted_s,
    latent_s,
    normed_s,
    halo_s,
    q_s,
    k_s,
    v_s,
    kh_s,
    vh_s,
    mixed_s,
    back_s,
    own_sem,
    send1,
    sendm1,
    recv1,
    recvm1,
    send2,
    sendm2,
    recv2,
    recvm2,
    send3,
    recv3,
):
    lon = lax.axis_index("lon")
    lat = lax.axis_index("lat")
    lon_next, lon_prev = lax.rem(lon + 1, n_lon), lax.rem(lon + n_lon - 1, n_lon)
    lat_next, lat_prev = lax.rem(lat + 1, n_lat), lax.rem(lat + n_lat - 1, n_lat)
    slab = 2 * n_lon

    barrier = pltpu.get_barrier_semaphore()

    def greet_lon(k, _):
        pl.semaphore_signal(barrier, inc=1, device_id={"lon": lax.rem(lon + k, n_lon)}, device_id_type=MESH)
        return 0

    def greet_lat(k, _):
        pl.semaphore_signal(barrier, inc=1, device_id={"lat": lax.rem(lat + k, n_lat)}, device_id_type=MESH)
        return 0

    lax.fori_loop(1, n_lon, greet_lon, 0)
    lax.fori_loop(1, n_lat, greet_lat, 0)
    for a in (lat_prev, lat_next):
        for b in (lon_prev, lon_next):
            pl.semaphore_signal(barrier, inc=1, device_id={"lon": b, "lat": a}, device_id_type=MESH)

    count = count_ref[...]
    rows = [[], [], []]
    for slot in range(2):
        place = place_of(cell_ref[:, slot, :].astype(jnp.float32))
        high = jnp.floor(place * (1.0 / 16.0))
        rows[0].append(jnp.where(count > slot, high, -32.0))
        rows[1].append(place - 16.0 * high)
        rows[2].append(instr_ref[:, slot, :].astype(jnp.float32))
    stacked = jnp.concatenate(rows[0] + rows[1] + rows[2], axis=0).astype(jnp.bfloat16)
    wide_in = 6 * n_lat
    eye = (
        lax.broadcasted_iota(jnp.int32, (wide_in, 128), 0) == lax.broadcasted_iota(jnp.int32, (wide_in, 128), 1)
    ).astype(jnp.float32).astype(jnp.bfloat16)
    meta_s[:, 0, :] = dot_tn(stacked, eye)

    pl.semaphore_wait(barrier, n_lon - 1 + n_lat - 1 + 4)

    def send_lon(k, _):
        to = lax.rem(lon + k, n_lon)
        pltpu.make_async_remote_copy(
            src_ref=meta_s.at[to],
            dst_ref=meta_r.at[lon],
            send_sem=sendm1,
            recv_sem=recvm1,
            device_id={"lon": to},
            device_id_type=MESH,
        ).start()
        pltpu.make_async_remote_copy(
            src_ref=values_hbm.at[to],
            dst_ref=buf1.at[lon],
            send_sem=send1,
            recv_sem=recv1,
            device_id={"lon": to},
            device_id_type=MESH,
        ).start()
        return 0

    lax.fori_loop(1, n_lon, send_lon, 0)
    own1 = pltpu.make_async_copy(values_hbm.at[lon], buf1.at[lon], own_sem.at[0])
    own1.start()
    ownm1 = pltpu.make_async_copy(meta_s.at[lon], meta_r.at[lon], own_sem.at[1])
    ownm1.start()

    lifted_s[:, 384:512] = jnp.ones((n_lat * slab, 128), jnp.bfloat16)
    back_s[...] = dot_nn(perm_ref[...], back_ref[...])

    def wait_bytes(ref, sem):
        pltpu.make_async_copy(ref, ref, sem).wait()

    ownm1.wait()
    wait_bytes(meta_r.at[pl.ds(0, n_lon - 1)], recvm1)
    meta = meta_r[:, 0, :].astype(jnp.bfloat16)
    source = lax.broadcasted_iota(jnp.int32, (n_lon, slab), 0)
    lane = lax.broadcasted_iota(jnp.int32, (n_lon, slab), 1)
    slots = []
    for slot in range(2):
        spread = (lane == 2 * source + slot).astype(jnp.float32).astype(jnp.bfloat16)
        slots.append(dot_tn(meta, spread))
    for kind in range(3):
        first = kind * 2 * n_lat
        meta2_s[:, kind, 0:slab] = slots[0][first : first + n_lat] + slots[1][first + n_lat : first + 2 * n_lat]

    own1.wait()
    wait_bytes(buf1.at[pl.ds(0, n_lon - 1)], recv1)

    def send_lat(k, _):
        to = lax.rem(lat + k, n_lat)
        pltpu.make_async_remote_copy(
            src_ref=meta2_s.at[to],
            dst_ref=meta2_r.at[lat],
            send_sem=sendm2,
            recv_sem=recvm2.at[lat],
            device_id={"lat": to},
            device_id_type=MESH,
        ).start()
        pltpu.make_async_remote_copy(
            src_ref=buf1.at[:, to],
            dst_ref=buf2.at[lat],
            send_sem=send2,
            recv_sem=recv2.at[lat],
            device_id={"lat": to},
            device_id_type=MESH,
        ).start()
        return 0

    lax.fori_loop(1, n_lat, send_lat, 0)
    pltpu.make_async_copy(buf1.at[:, lat], buf2.at[lat], recv2.at[lat]).start()
    pltpu.make_async_copy(meta2_s.at[lat], meta2_r.at[lat], recvm2.at[lat]).start()

    def encode(k, _):
        came = lax.rem(lat + n_lat - k, n_lat)
        wait_bytes(meta2_r.at[came], recvm2.at[came])
        wait_bytes(buf2.at[came], recv2.at[came])
        info = meta2_r[came]
        info = info[:, 0:slab]
        place = info[0:1] * 16.0 + info[1:2]
        cells = lax.broadcasted_iota(jnp.int32, (CELLS, slab), 0).astype(jnp.float32)
        at = pl.multiple_of(k * slab, slab)
        onehot_s[:, pl.ds(at, slab)] = (cells == place).astype(jnp.float32).astype(jnp.bfloat16)
        tags = lax.broadcasted_iota(jnp.int32, (INSTR, slab), 0).astype(jnp.float32)
        chooser = (tags == info[2:3]).astype(jnp.float32).astype(jnp.bfloat16)
        records = buf2[came].reshape(slab, 128)
        before = dot_nt(records, win_ref[...]) + dot_tn(chooser, table_ref[...])
        encoded = gelu(before).astype(jnp.bfloat16)
        lifted = gelu(dot_nn(encoded, lift_ref[...])).astype(jnp.bfloat16)
        lifted_s[pl.ds(at, slab), 0:384] = lifted
        return 0

    lax.fori_loop(0, n_lat, encode, 0)

    total = dot_nn(onehot_s[...], lifted_s[...])
    tally = 1.0 + total[:, 384:385]
    mean = (back_s[...] + total[:, 0:384]) / tally
    parts = []
    for name, _, _ in ORDER:
        at, _, padded = PIECES[name]
        parts += [mean[at : at + padded, 0:192], mean[at : at + padded, 192:384]]
    latent = jnp.concatenate(parts, axis=0).astype(jnp.bfloat16)
    latent_s[...] = latent
    normed_s[...] = norm(latent.astype(jnp.float32), gain1_ref[...].astype(jnp.float32))

    def rows_of(name):
        at, _, padded = PIECES[name]
        return LEV * at, LEV * padded

    def span(first, last):
        a, _ = rows_of(first)
        b, size = rows_of(last)
        return a, b + size - a

    up_to = {"lat": lat_prev}
    down_to = {"lat": lat_next}
    sends = [
        (span("c00", "c03"), 0, up_to),
        (span("c03", "c33"), 176, {"lon": lon_next}),
        (span("c33", "c30"), 352, down_to),
        (span("c30", "L"), 528, {"lon": lon_prev}),
        (span("c00", "c00"), 656, {"lon": lon_prev}),
        (span("c00", "c00"), 704, {"lon": lon_prev, "lat": lat_prev}),
        (span("c03", "c03"), 752, {"lon": lon_next, "lat": lat_prev}),
        (span("c33", "c33"), 800, {"lon": lon_next, "lat": lat_next}),
        (span("c30", "c30"), 848, {"lon": lon_prev, "lat": lat_next}),
    ]
    copies = []
    for index, ((at, size), there, device) in enumerate(sends):
        copy = pltpu.make_async_remote_copy(
            src_ref=normed_s.at[pl.ds(at, size)],
            dst_ref=halo_s.at[pl.ds(there, size)],
            send_sem=send3.at[index],
            recv_sem=recv3.at[index],
            device_id=device,
            device_id_type=MESH,
        )
        copy.start()
        copies.append(copy)

    normed = normed_s[...]
    q_s[...] = (dot_nn(normed, attn_ref[:, 0:192]) * (32.0**-0.5)).astype(jnp.bfloat16)
    k_s[...] = dot_nn(normed, attn_ref[:, 192:384]).astype(jnp.bfloat16)
    v_s[...] = dot_nn(normed, attn_ref[:, 384:576]).astype(jnp.bfloat16)

    def heads_of(shape):
        return lax.broadcasted_iota(jnp.int32, shape, 1) // 32

    def attend(name, keys, values, bias):
        at, size = rows_of(name)
        query = q_s[pl.ds(at, size), :]
        head = heads_of((size, 192))
        stack = jnp.concatenate([jnp.where(head == h, query, jnp.zeros_like(query)) for h in range(HEADS)], axis=0)
        scores = dot_nt(stack, keys)
        if bias is not None:
            scores = scores + bias
        largest = jnp.max(scores, axis=-1, keepdims=True)
        raised = jnp.exp(scores - largest)
        weights = (raised / jnp.sum(raised, axis=-1, keepdims=True)).astype(jnp.bfloat16)
        output = dot_nn(weights, values)
        merged = output[0:size]
        for h in range(1, HEADS):
            merged = jnp.where(head == h, output[h * size : (h + 1) * size], merged)
        mixed_s[pl.ds(at, size), :] = merged.astype(jnp.bfloat16)

    at, size = rows_of("C")
    attend("C", k_s[pl.ds(at, size), :], v_s[pl.ds(at, size), :], None)

    for copy in copies:
        copy.wait_recv()
    halo = halo_s[...]
    kh_s[...] = dot_nn(halo, attn_ref[:, 192:384]).astype(jnp.bfloat16)
    vh_s[...] = dot_nn(halo, attn_ref[:, 384:576]).astype(jnp.bfloat16)

    windows = [
        ("T", [(400, 80)], lat == 0),
        ("B", [(48, 80)], lat == n_lat - 1),
        ("L", [(224, 80)], None),
        ("R", [(576, 80)], None),
        ("c00", [(176, 48), (480, 48), (800, 48)], lat == 0),
        ("c03", [(656, 48), (352, 48), (848, 48)], lat == 0),
        ("c30", [(304, 48), (0, 48), (752, 48)], lat == n_lat - 1),
        ("c33", [(528, 48), (128, 48), (704, 48)], lat == n_lat - 1),
    ]
    for name, others, edge in windows:
        at, size = rows_of(name)
        _, cells, padded = PIECES[name]
        count = size * (1 + len(others))
        keys = jnp.concatenate([k_s[pl.ds(at, size), :]] + [kh_s[pl.ds(a, n), :] for a, n in others], axis=0)
        values = jnp.concatenate([v_s[pl.ds(at, size), :]] + [vh_s[pl.ds(a, n), :] for a, n in others], axis=0)
        lane = lax.broadcasted_iota(jnp.int32, (1, count), 1)
        live = lax.rem(lane, padded) < cells
        if edge is not None:
            live = live & ((lane < count // 2) | jnp.logical_not(edge))
        attend(name, keys, values, jnp.where(live, 0.0, FAR))

    after = (latent_s[...].astype(jnp.float32) + dot_nn(mixed_s[...], mix_ref[...])).astype(jnp.bfloat16)
    after = after.astype(jnp.float32)
    normed_two = norm(after, gain2_ref[...].astype(jnp.float32))
    hidden = gelu(dot_nn(normed_two, up_ref[...])).astype(jnp.bfloat16)
    result = after + dot_nt(hidden, down_ref[...])
    for level in range(LEV):
        parts = []
        for name, _, _ in ORDER:
            at, size = rows_of(name)
            parts.append(result[at + level * (size // 2) : at + (level + 1) * (size // 2)])
        whole = jnp.concatenate(parts, axis=0).astype(jnp.bfloat16)
        out_ref[:, level * 192 : (level + 1) * 192] = dot_tn(perm_ref[...], whole).astype(jnp.bfloat16)

    wait_bytes(meta_s.at[pl.ds(0, n_lon - 1)], sendm1)
    wait_bytes(buf1.at[pl.ds(0, n_lon - 1)], send1)
    wait_bytes(meta2_s.at[pl.ds(0, n_lat - 1)], sendm2)
    wait_bytes(buf2.at[pl.ds(0, n_lat - 1)], send2)
    for copy in copies:
        copy.wait_send()


def local(
    n_lon,
    n_lat,
    record_values,
    record_cell,
    record_instrument,
    block_counts,
    background,
    input_weight,
    instrument_table,
    lift_weight,
    first_gain,
    attn_weight,
    mix_weight,
    second_gain,
    up_weight,
    down_weight,
):
    vmem = pl.BlockSpec(memory_space=pltpu.VMEM)
    perm = jnp.asarray(cell_permutation(), jnp.bfloat16)
    slab = 2 * n_lon
    out = pl.pallas_call(
        functools.partial(kernel, n_lon, n_lat),
        out_shape=jax.ShapeDtypeStruct((288, 384), jnp.bfloat16),
        in_specs=[pl.BlockSpec(memory_space=pl.ANY)] + [vmem] * 14,
        out_specs=vmem,
        scratch_shapes=[
            pltpu.VMEM((n_lon, n_lat, 2, 128), jnp.bfloat16),
            pltpu.VMEM((n_lat, n_lon, 2, 128), jnp.bfloat16),
            pltpu.VMEM((n_lon, 1, 128), jnp.float32),
            pltpu.VMEM((n_lon, 1, 128), jnp.float32),
            pltpu.VMEM((n_lat, 8, 128), jnp.float32),
            pltpu.VMEM((n_lat, 8, 128), jnp.float32),
            pltpu.VMEM((CELLS, n_lat * slab), jnp.bfloat16),
            pltpu.VMEM((n_lat * slab, 512), jnp.bfloat16),
            pltpu.VMEM((TOKENS, 192), jnp.bfloat16),
            pltpu.VMEM((TOKENS, 192), jnp.bfloat16),
            pltpu.VMEM((HALO, 192), jnp.bfloat16),
            pltpu.VMEM((TOKENS, 192), jnp.bfloat16),
            pltpu.VMEM((TOKENS, 192), jnp.bfloat16),
            pltpu.VMEM((TOKENS, 192), jnp.bfloat16),
            pltpu.VMEM((HALO, 192), jnp.bfloat16),
            pltpu.VMEM((HALO, 192), jnp.bfloat16),
            pltpu.VMEM((TOKENS, 192), jnp.bfloat16),
            pltpu.VMEM((CELLS, 384), jnp.float32),
            pltpu.SemaphoreType.DMA((2,)),
            pltpu.SemaphoreType.DMA,
            pltpu.SemaphoreType.DMA,
            pltpu.SemaphoreType.DMA,
            pltpu.SemaphoreType.DMA,
            pltpu.SemaphoreType.DMA,
            pltpu.SemaphoreType.DMA,
            pltpu.SemaphoreType.DMA((n_lat,)),
            pltpu.SemaphoreType.DMA((n_lat,)),
            pltpu.SemaphoreType.DMA((9,)),
            pltpu.SemaphoreType.DMA((9,)),
        ],
        compiler_params=pltpu.CompilerParams(
            collective_id=0, has_side_effects=True, vmem_limit_bytes=40 * 1024 * 1024
        ),
    )(
        record_values,
        record_cell.transpose(1, 2, 0),
        record_instrument.transpose(1, 2, 0),
        block_counts.transpose(1, 0),
        background.reshape(288, 384),
        perm,
        input_weight.T,
        instrument_table,
        lift_weight,
        first_gain.reshape(1, 192),
        attn_weight,
        mix_weight,
        second_gain.reshape(1, 192),
        up_weight,
        down_weight.T,
    )
    return out.reshape(12, 24, 2, 192)


def solution(mesh):
    placed = (
        P("lon", "lat", None, None),
        P("lon", "lat", None),
        P("lon", "lat", None),
        P("lon", "lat"),
        P("lat", "lon", None, None),
    ) + (P(),) * 9
    return jax.shard_map(
        functools.partial(local, mesh.shape["lon"], mesh.shape["lat"]),
        mesh=mesh,
        in_specs=placed,
        out_specs=P("lat", "lon", None, None),
        check_vma=False,
    )
```

time: 213 us -> 91.3 us (0.43)
  the two profiles are of different devices: /device:TPU:32 before, /device:TPU:3 now
where the time goes in v1:
time: 91.3 us; the launch traced here: 90.7 us
  Pallas kernels  78.7 us (86%)
  local copies, waits for them, and re-layouts  12 us (13%)
    pallas_call x1, Pallas kernels, local(): pl.pallas_call(functools.partial(kernel, n_lon, n_lat), out_shape=jax.Sha...  78.7 us
    unnamed x24, local copies, waits for them, and re-layouts  8.54 us

profile of v1, /device:TPU:3, one launch (start us, length us, event | category | flops | bytes accessed | tf_op | source)
XLA Modules:
  0.0 90.7 jit_solution(10131021846410910572)
XLA Ops:
  0.0 0.0 copy-start
  0.0 0.7 reshape.13.gain1_ref
  0.7 0.7 reshape.14.gain2_ref
  1.4 0.0 copy-start.11
  1.4 1.2 %reshape.12.back_ref = bf16[288,384]{1,0:T(8,128)(2,1)S(1)} reshape(bf16[12,24,2,192]{3,2,1,0:T(2,128)(2,1)} %param.19) | data formatting | bytes 442368 | tf_op jit(solution)/shard_map/reshape | solution.py:460
  2.6 0.0 copy-done
  2.6 0.0 copy-done.11
  2.6 0.0 copy-start.1
  2.6 1.0 %copy-done.1 = bf16[192,768]{1,0:T(8,128)(2,1)S(1)} copy-done((bf16[192,768]{1,0:T(8,128)(2,1)S(1)}, bf16[192,768]{1,0:T(8,128)(2,1)}, u32[]{:S(2)}) %copy-start.1) | copy-done | bytes 294936
  3.5 0.0 copy-start.2
  3.6 1.0 %copy-done.2 = bf16[768,192]{0,1:T(8,128)(2,1)S(1)} copy-done((bf16[768,192]{0,1:T(8,128)(2,1)S(1)}, bf16[768,192]{0,1:T(8,128)(2,1)}, u32[]{:S(2)}) %copy-start.2) | copy-done | bytes 294936
  4.5 0.0 copy-start.3
  4.5 0.9 %copy-done.3 = bf16[328,288]{1,0:T(8,128)(2,1)S(1)} copy-done((bf16[328,288]{1,0:T(8,128)(2,1)S(1)}, bf16[328,288]{1,0:T(8,128)(2,1)}, u32[]{:S(2)}) %copy-start.3) | copy-done | bytes 188952
  5.5 0.0 copy-start.4
  5.5 0.9 %copy-done.4 = bf16[192,576]{1,0:T(8,128)(2,1)S(1)} copy-done((bf16[192,576]{1,0:T(8,128)(2,1)S(1)}, bf16[192,576]{1,0:T(8,128)(2,1)}, u32[]{:S(2)}) %copy-start.4) | copy-done | bytes 221208
  6.4 0.0 copy-start.5
  6.4 0.9 %copy-done.5 = bf16[192,384]{1,0:T(8,128)(2,1)S(1)} copy-done((bf16[192,384]{1,0:T(8,128)(2,1)S(1)}, bf16[192,384]{1,0:T(8,128)(2,1)}, u32[]{:S(2)}) %copy-start.5) | copy-done | bytes 147480
  7.3 0.0 copy-start.6
  7.3 0.9 copy-done.6
  8.2 0.0 copy-start.7
  8.2 0.8 copy-done.7
  9.0 0.0 copy-start.8
  9.0 0.7 copy-done.8
  9.7 0.0 copy-start.9
  9.7 0.7 copy-done.9
  10.4 0.0 copy-start.10
  10.4 0.7 copy-done.10
  11.1 78.7 %shard_map.145 = bf16[288,384]{1,0:T(8,128)(2,1)S(1)} custom-call(bf16[64,16,2,128]{3,2,1,0:T(2,128)(2,1)S(1)} %copy-done, s32[16,2,64]{2,1,0:T(2,128)S(1)} %bitcast.7, s32[16,2,64]{2,1,0:T(2,128)S(1)} %bitcast.8, s32[16,64]{1,0:T(8,128)S(1)} %bitcast.9, bf16[288,384]{1,0:T(8,128)(2,1)S(1)} %reshape.12.back_ref, bf16[328,288]{1,0:T(8,128)(2,1)S(1)} %copy-done.3, ...), custom_call_target="tpu_custom_call" | custom-call | tf_op jit(solution)/shard_map/pallas_call | solution.py:416
  89.8 0.9 reshape.15
Async XLA Ops:
  0.0 2.6 %copy-start = (bf16[64,16,2,128]{3,2,1,0:T(2,128)(2,1)S(1)}, bf16[64,16,2,128]{3,2,1,0:T(2,128)(2,1)}, u32[]{:S(2)}) copy-start(bf16[64,16,2,128]{3,2,1,0:T(2,128)(2,1)} %values_hbm.1) | copy-start | bytes 1572868
  1.4 1.2 %copy-start.11 = (bf16[8,192]{1,0:T(8,128)(2,1)S(1)}, bf16[8,192]{1,0:T(8,128)(2,1)}, u32[]{:S(2)}) copy-start(bf16[8,192]{1,0:T(8,128)(2,1)} %table_ref.1) | copy-start | bytes 9220
  2.6 1.0 %copy-start.1 = (bf16[192,768]{1,0:T(8,128)(2,1)S(1)}, bf16[192,768]{1,0:T(8,128)(2,1)}, u32[]{:S(2)}) copy-start(bf16[192,768]{1,0:T(8,128)(2,1)} %up_ref.1) | copy-start | bytes 884740
  3.5 1.0 %copy-start.2 = (bf16[768,192]{0,1:T(8,128)(2,1)S(1)}, bf16[768,192]{0,1:T(8,128)(2,1)}, u32[]{:S(2)}) copy-start(bf16[768,192]{0,1:T(8,128)(2,1)} %param.28) | copy-start | bytes 884740
  4.5 0.9 %copy-start.3 = (bf16[328,288]{1,0:T(8,128)(2,1)S(1)}, bf16[328,288]{1,0:T(8,128)(2,1)}, u32[]{:S(2)}) copy-start(bf16[328,288]{1,0:T(8,128)(2,1)} %constant.2.clone.perm_ref) | copy-start | bytes 566788
  5.5 0.9 %copy-start.4 = (bf16[192,576]{1,0:T(8,128)(2,1)S(1)}, bf16[192,576]{1,0:T(8,128)(2,1)}, u32[]{:S(2)}) copy-start(bf16[192,576]{1,0:T(8,128)(2,1)} %attn_ref.1) | copy-start | bytes 663556
  6.4 0.9 %copy-start.5 = (bf16[192,384]{1,0:T(8,128)(2,1)S(1)}, bf16[192,384]{1,0:T(8,128)(2,1)}, u32[]{:S(2)}) copy-start(bf16[192,384]{1,0:T(8,128)(2,1)} %lift_ref.1) | copy-start | bytes 442372
  7.3 0.9 copy-start.6
  8.2 0.8 copy-start.7
  9.0 0.7 copy-start.8
  9.7 0.7 copy-start.9
  10.4 0.7 copy-start.10

commit v2 on v1

--- a/solution.py
+++ b/solution.py
@@ -34,23 +34,11 @@
 PIECES, CELLS = piece_table()
 TOKENS = LEV * CELLS
 HALO = 896
-WIDE = 448
 
 
 def base_of(i, j):
     name = [n for n, a, b in ORDER if (a, b) == (i, j)][0]
     return PIECES[name][0]
-
-
-def cell_permutation():
-    matrix = np.zeros((CELLS, 288), np.float32)
-    for _, i, j in ORDER:
-        breadth = COL_CUTS[j + 1] - COL_CUTS[j]
-        for r in range(ROW_CUTS[i], ROW_CUTS[i + 1]):
-            for c in range(COL_CUTS[j], COL_CUTS[j + 1]):
-                place = base_of(i, j) + (r - ROW_CUTS[i]) * breadth + c - COL_CUTS[j]
-                matrix[place, r * 24 + c] = 1.0
-    return matrix
 
 
 def dot_nn(a, b):
@@ -88,15 +76,44 @@
     return place
 
 
+def token_of(source):
+    cell = jnp.floor((source + 0.5) * 0.5)
+    level = source - 2.0 * cell
+    place = place_of(cell)
+    token = jnp.zeros_like(source)
+    for name, _, _ in ORDER:
+        at, _, padded = PIECES[name]
+        token = jnp.where(place >= at, place + at + level * padded, token)
+    return token
+
+
+def grid_of(n_lon, n_lat):
+    n_yl, n_x = (4, 8) if n_lon == 64 else (2, 2)
+    return n_yl, n_x, n_lon // (n_yl * n_x), 2, n_lat // 2
+
+
 def kernel(
     n_lon,
     n_lat,
     values_hbm,
+    cell_hbm,
+    instr_hbm,
+    count_hbm,
+    back_hbm,
+    win_hbm,
+    table_hbm,
+    lift_hbm,
+    gain1_hbm,
+    attn_hbm,
+    mix_hbm,
+    gain2_hbm,
+    up_hbm,
+    down_hbm,
+    out_ref,
     cell_ref,
     instr_ref,
     count_ref,
     back_ref,
-    perm_ref,
     win_ref,
     table_ref,
     lift_ref,
@@ -106,8 +123,11 @@
     gain2_ref,
     up_ref,
     down_ref,
-    out_ref,
-    buf1,
+    perm_s,
+    turn_s,
+    load_sem,
+    buf_a,
+    buf_b,
     buf2,
     meta_s,
     meta_r,
@@ -126,11 +146,14 @@
     mixed_s,
     back_s,
     own_sem,
-    send1,
+    send_a,
+    send_b,
+    send_a2,
+    send_b2,
     sendm1,
-    recv1,
+    recv_a,
+    recv_b,
     recvm1,
-    send2,
     sendm2,
     recv2,
     recvm2,
@@ -142,6 +165,23 @@
     lon_next, lon_prev = lax.rem(lon + 1, n_lon), lax.rem(lon + n_lon - 1, n_lon)
     lat_next, lat_prev = lax.rem(lat + 1, n_lat), lax.rem(lat + n_lat - 1, n_lat)
     slab = 2 * n_lon
+    n_yl, n_x, n_c, n_yh, n_z = grid_of(n_lon, n_lat)
+    core, x, yl = lax.rem(lon, n_c), lax.rem(lon // n_c, n_x), lon // (n_c * n_x)
+    z, yh = lax.rem(lat, n_z), lat // n_z
+    n_a, n_b = n_yh * n_yl * n_c, n_x * n_z
+
+    def lon_of(a, b, c):
+        return (a * n_x + b) * n_c + c
+
+    def peer_a(k):
+        i = lax.rem((yh * n_yl + yl) * n_c + core + k, n_a)
+        to_c, to_yl, to_yh = lax.rem(i, n_c), lax.rem(i // n_c, n_yl), i // (n_c * n_yl)
+        return to_yh, to_yl, to_c, {"lon": lon_of(to_yl, x, to_c), "lat": to_yh * n_z + z}
+
+    def peer_b(k):
+        i = lax.rem(x * n_z + z + k, n_b)
+        to_z, to_x = lax.rem(i, n_z), i // n_z
+        return to_x, to_z, {"lon": lon_of(yl, to_x, core), "lat": yh * n_z + to_z}
 
     barrier = pltpu.get_barrier_semaphore()
 
@@ -153,12 +193,95 @@
         pl.semaphore_signal(barrier, inc=1, device_id={"lat": lax.rem(lat + k, n_lat)}, device_id_type=MESH)
         return 0
 
+    def greet_a(k, _):
+        pl.semaphore_signal(barrier, inc=1, device_id=peer_a(k)[-1], device_id_type=MESH)
+        return 0
+
+    def greet_b(k, _):
+        pl.semaphore_signal(barrier, inc=1, device_id=peer_b(k)[-1], device_id_type=MESH)
+        return 0
+
+    lax.fori_loop(1, n_b, greet_b, 0)
+    lax.fori_loop(1, n_a, greet_a, 0)
     lax.fori_loop(1, n_lon, greet_lon, 0)
     lax.fori_loop(1, n_lat, greet_lat, 0)
     for a in (lat_prev, lat_next):
         for b in (lon_prev, lon_next):
             pl.semaphore_signal(barrier, inc=1, device_id={"lon": b, "lat": a}, device_id_type=MESH)
 
+    loads = []
+    pairs = (
+        (cell_hbm, cell_ref),
+        (instr_hbm, instr_ref),
+        (count_hbm, count_ref),
+        (back_hbm, back_ref),
+        (win_hbm, win_ref),
+        (table_hbm, table_ref),
+        (lift_hbm, lift_ref),
+        (gain1_hbm, gain1_ref),
+        (attn_hbm, attn_ref),
+        (mix_hbm, mix_ref),
+        (gain2_hbm, gain2_ref),
+        (up_hbm, up_ref),
+        (down_hbm, down_ref),
+    )
+    for index, (source, target) in enumerate(pairs):
+        load = pltpu.make_async_copy(source, target, load_sem.at[index])
+        load.start()
+        loads.append(load)
+
+    pl.semaphore_wait(barrier, n_a - 1 + n_b - 1 + n_lon - 1 + n_lat - 1 + 4)
+
+    def send_lon(k, _):
+        to = lax.rem(lon + k, n_lon)
+        pltpu.make_async_remote_copy(
+            src_ref=meta_s.at[to],
+            dst_ref=meta_r.at[lon],
+            send_sem=sendm1,
+            recv_sem=recvm1,
+            device_id={"lon": to},
+            device_id_type=MESH,
+        ).start()
+        return 0
+
+    def block_a(to_yh, to_yl, to_c):
+        odd = lax.rem(to_yl, 2)
+        return values_hbm.at[to_yl // 2, odd, :, odd, to_c, to_yh]
+
+    def block_b(to_x, to_z):
+        odd = lax.rem(to_x, 2)
+        return values_hbm.at[:, 1 - odd, to_x // 2, odd, :, :, to_z]
+
+    def send_first_a(k, _):
+        to_yh, to_yl, to_c, device = peer_a(k)
+        pltpu.make_async_remote_copy(
+            src_ref=block_a(to_yh, to_yl, to_c),
+            dst_ref=buf_a.at[yh, yl, core],
+            send_sem=send_a.at[k],
+            recv_sem=recv_a,
+            device_id=device,
+            device_id_type=MESH,
+        ).start()
+        return 0
+
+    def send_first_b(k, _):
+        to_x, to_z, device = peer_b(k)
+        pltpu.make_async_remote_copy(
+            src_ref=block_b(to_x, to_z),
+            dst_ref=buf_b.at[z, x],
+            send_sem=send_b.at[k],
+            recv_sem=recv_b,
+            device_id=device,
+            device_id_type=MESH,
+        ).start()
+        return 0
+
+    lax.fori_loop(1, n_a, send_first_a, 0)
+    lax.fori_loop(1, n_b, send_first_b, 0)
+    pltpu.make_async_copy(block_a(yh, yl, core), buf_a.at[yh, yl, core], recv_a).start()
+    pltpu.make_async_copy(block_b(x, z), buf_b.at[z, x], recv_b).start()
+    for load in loads[:3]:
+        load.wait()
     count = count_ref[...]
     rows = [[], [], []]
     for slot in range(2):
@@ -174,40 +297,84 @@
     ).astype(jnp.float32).astype(jnp.bfloat16)
     meta_s[:, 0, :] = dot_tn(stacked, eye)
 
-    pl.semaphore_wait(barrier, n_lon - 1 + n_lat - 1 + 4)
-
-    def send_lon(k, _):
-        to = lax.rem(lon + k, n_lon)
-        pltpu.make_async_remote_copy(
-            src_ref=meta_s.at[to],
-            dst_ref=meta_r.at[lon],
-            send_sem=sendm1,
-            recv_sem=recvm1,
-            device_id={"lon": to},
-            device_id_type=MESH,
-        ).start()
-        pltpu.make_async_remote_copy(
-            src_ref=values_hbm.at[to],
-            dst_ref=buf1.at[lon],
-            send_sem=send1,
-            recv_sem=recv1,
-            device_id={"lon": to},
-            device_id_type=MESH,
-        ).start()
-        return 0
-
     lax.fori_loop(1, n_lon, send_lon, 0)
-    own1 = pltpu.make_async_copy(values_hbm.at[lon], buf1.at[lon], own_sem.at[0])
-    own1.start()
     ownm1 = pltpu.make_async_copy(meta_s.at[lon], meta_r.at[lon], own_sem.at[1])
     ownm1.start()
 
+    normed_s[...] = jnp.zeros_like(normed_s)
     lifted_s[:, 384:512] = jnp.ones((n_lat * slab, 128), jnp.bfloat16)
-    back_s[...] = dot_nn(perm_ref[...], back_ref[...])
+    token_row = token_of(lax.broadcasted_iota(jnp.int32, (1, 576), 1).astype(jnp.float32))
+    token_at = lax.broadcasted_iota(jnp.int32, (TOKENS, 576), 0).astype(jnp.float32)
+    perm_s[...] = (token_at == token_row).astype(jnp.float32).astype(jnp.bfloat16)
+    token_col = token_of(lax.broadcasted_iota(jnp.int32, (576, 1), 0).astype(jnp.float32))
+    token_on = lax.broadcasted_iota(jnp.int32, (576, TOKENS), 1).astype(jnp.float32)
+    turn_s[...] = (token_on == token_col).astype(jnp.float32).astype(jnp.bfloat16)
+    for load in loads[3:]:
+        load.wait()
+    back_s[...] = dot_nn(perm_s[...], back_ref[...].reshape(576, 192))
 
     def wait_bytes(ref, sem):
         pltpu.make_async_copy(ref, ref, sem).wait()
 
+    odd_x, odd_y = lax.rem(x, 2), lax.rem(yl, 2)
+    half_x, half_y = n_x // 2, n_yl // 2
+    n_a2, n_b2 = half_y * n_yh * n_c, half_x * n_z
+    mine_a = (yh * half_y + yl // 2) * n_c + core
+    mine_b = (x // 2) * n_z + z
+
+    def second_b(k):
+        i = lax.rem(mine_b + k, n_b2)
+        half, to_z = i // n_z, lax.rem(i, n_z)
+        device = {"lon": lon_of(yl, 2 * half + odd_y, core), "lat": yh * n_z + to_z}
+        return buf_a.at[:, :, :, half, to_z], buf2.at[:, z, :, x], device
+
+    def second_a(k):
+        i = lax.rem(mine_a + k, n_a2)
+        to_c, half, to_yh = lax.rem(i, n_c), lax.rem(i // n_c, half_y), i // (n_c * half_y)
+        device = {"lon": lon_of(2 * half + 1 - odd_x, x, to_c), "lat": to_yh * n_z + z}
+        return buf_b.at[:, :, half, to_c, to_yh], buf2.at[yh, :, yl, :, core], device
+
+    def send_second(part, sem):
+        def send(k, _):
+            source, target, device = part(k)
+            pltpu.make_async_remote_copy(
+                src_ref=source,
+                dst_ref=target,
+                send_sem=sem.at[k],
+                recv_sem=recv2,
+                device_id=device,
+                device_id_type=MESH,
+            ).start()
+            return 0
+
+        return send
+
+    even = odd_x == odd_y
+
+    wait_bytes(buf_b, recv_b)
+
+    @pl.when(even)
+    def _():
+        send_second(second_a, send_a2)(0, 0)
+
+    @pl.when(jnp.logical_not(even))
+    def _():
+        source, target, _ = second_a(0)
+        pltpu.make_async_copy(source, target, recv2).start()
+
+    lax.fori_loop(1, n_a2, send_second(second_a, send_a2), 0)
+    wait_bytes(buf_a, recv_a)
+
+    @pl.when(jnp.logical_not(even))
+    def _():
+        send_second(second_b, send_b2)(0, 0)
+
+    @pl.when(even)
+    def _():
+        source, target, _ = second_b(0)
+        pltpu.make_async_copy(source, target, recv2).start()
+
+    lax.fori_loop(1, n_b2, send_second(second_b, send_b2), 0)
     ownm1.wait()
     wait_bytes(meta_r.at[pl.ds(0, n_lon - 1)], recvm1)
     meta = meta_r[:, 0, :].astype(jnp.bfloat16)
@@ -221,8 +388,6 @@
         first = kind * 2 * n_lat
         meta2_s[:, kind, 0:slab] = slots[0][first : first + n_lat] + slots[1][first + n_lat : first + 2 * n_lat]
 
-    own1.wait()
-    wait_bytes(buf1.at[pl.ds(0, n_lon - 1)], recv1)
 
     def send_lat(k, _):
         to = lax.rem(lat + k, n_lat)
@@ -234,25 +399,17 @@
             device_id={"lat": to},
             device_id_type=MESH,
         ).start()
-        pltpu.make_async_remote_copy(
-            src_ref=buf1.at[:, to],
-            dst_ref=buf2.at[lat],
-            send_sem=send2,
-            recv_sem=recv2.at[lat],
-            device_id={"lat": to},
-            device_id_type=MESH,
-        ).start()
         return 0
 
     lax.fori_loop(1, n_lat, send_lat, 0)
-    pltpu.make_async_copy(buf1.at[:, lat], buf2.at[lat], recv2.at[lat]).start()
     pltpu.make_async_copy(meta2_s.at[lat], meta2_r.at[lat], recvm2.at[lat]).start()
 
+    for came in range(n_lat):
+        wait_bytes(meta2_r.at[came], recvm2.at[came])
+    wait_bytes(buf2, recv2)
+
     def encode(k, _):
-        came = lax.rem(lat + n_lat - k, n_lat)
-        wait_bytes(meta2_r.at[came], recvm2.at[came])
-        wait_bytes(buf2.at[came], recv2.at[came])
-        info = meta2_r[came]
+        info = meta2_r[k]
         info = info[:, 0:slab]
         place = info[0:1] * 16.0 + info[1:2]
         cells = lax.broadcasted_iota(jnp.int32, (CELLS, slab), 0).astype(jnp.float32)
@@ -260,7 +417,7 @@
         onehot_s[:, pl.ds(at, slab)] = (cells == place).astype(jnp.float32).astype(jnp.bfloat16)
         tags = lax.broadcasted_iota(jnp.int32, (INSTR, slab), 0).astype(jnp.float32)
         chooser = (tags == info[2:3]).astype(jnp.float32).astype(jnp.bfloat16)
-        records = buf2[came].reshape(slab, 128)
+        records = buf2[k // n_z, lax.rem(k, n_z)].reshape(slab, 128)
         before = dot_nt(records, win_ref[...]) + dot_tn(chooser, table_ref[...])
         encoded = gelu(before).astype(jnp.bfloat16)
         lifted = gelu(dot_nn(encoded, lift_ref[...])).astype(jnp.bfloat16)
@@ -271,14 +428,15 @@
 
     total = dot_nn(onehot_s[...], lifted_s[...])
     tally = 1.0 + total[:, 384:385]
-    mean = (back_s[...] + total[:, 0:384]) / tally
-    parts = []
+    parts, tallies = [], []
     for name, _, _ in ORDER:
         at, _, padded = PIECES[name]
-        parts += [mean[at : at + padded, 0:192], mean[at : at + padded, 192:384]]
-    latent = jnp.concatenate(parts, axis=0).astype(jnp.bfloat16)
+        parts += [total[at : at + padded, 0:192], total[at : at + padded, 192:384]]
+        tallies += [tally[at : at + padded]] * 2
+    latent = (back_s[...] + jnp.concatenate(parts, axis=0)) / jnp.concatenate(tallies, axis=0)
+    latent = latent.astype(jnp.bfloat16)
     latent_s[...] = latent
-    normed_s[...] = norm(latent.astype(jnp.float32), gain1_ref[...].astype(jnp.float32))
+    normed_s[:, 0:192] = norm(latent.astype(jnp.float32), gain1_ref[...].reshape(1, 192).astype(jnp.float32))
 
     def rows_of(name):
         at, _, padded = PIECES[name]
@@ -315,7 +473,7 @@
         copy.start()
         copies.append(copy)
 
-    normed = normed_s[...]
+    normed = normed_s[:, 0:192]
     q_s[...] = (dot_nn(normed, attn_ref[:, 0:192]) * (32.0**-0.5)).astype(jnp.bfloat16)
     k_s[...] = dot_nn(normed, attn_ref[:, 192:384]).astype(jnp.bfloat16)
     v_s[...] = dot_nn(normed, attn_ref[:, 384:576]).astype(jnp.bfloat16)
@@ -345,7 +503,7 @@
 
     for copy in copies:
         copy.wait_recv()
-    halo = halo_s[...]
+    halo = halo_s[:, 0:192]
     kh_s[...] = dot_nn(halo, attn_ref[:, 192:384]).astype(jnp.bfloat16)
     vh_s[...] = dot_nn(halo, attn_ref[:, 384:576]).astype(jnp.bfloat16)
 
@@ -373,21 +531,43 @@
 
     after = (latent_s[...].astype(jnp.float32) + dot_nn(mixed_s[...], mix_ref[...])).astype(jnp.bfloat16)
     after = after.astype(jnp.float32)
-    normed_two = norm(after, gain2_ref[...].astype(jnp.float32))
+    normed_two = norm(after, gain2_ref[...].reshape(1, 192).astype(jnp.float32))
     hidden = gelu(dot_nn(normed_two, up_ref[...])).astype(jnp.bfloat16)
     result = after + dot_nt(hidden, down_ref[...])
-    for level in range(LEV):
-        parts = []
-        for name, _, _ in ORDER:
-            at, size = rows_of(name)
-            parts.append(result[at + level * (size // 2) : at + (level + 1) * (size // 2)])
-        whole = jnp.concatenate(parts, axis=0).astype(jnp.bfloat16)
-        out_ref[:, level * 192 : (level + 1) * 192] = dot_tn(perm_ref[...], whole).astype(jnp.bfloat16)
+    out_ref[...] = dot_nn(turn_s[...], result.astype(jnp.bfloat16)).astype(jnp.bfloat16)
 
     wait_bytes(meta_s.at[pl.ds(0, n_lon - 1)], sendm1)
-    wait_bytes(buf1.at[pl.ds(0, n_lon - 1)], send1)
     wait_bytes(meta2_s.at[pl.ds(0, n_lat - 1)], sendm2)
-    wait_bytes(buf2.at[pl.ds(0, n_lat - 1)], send2)
+
+    def done_first_a(k, _):
+        wait_bytes(buf_a.at[0, 0, 0], send_a.at[k])
+        return 0
+
+    def done_first_b(k, _):
+        wait_bytes(buf_b.at[0, 0], send_b.at[k])
+        return 0
+
+    def done_second_a(k, _):
+        wait_bytes(buf2.at[0, :, 0, :, 0], send_a2.at[k])
+        return 0
+
+    def done_second_b(k, _):
+        wait_bytes(buf2.at[:, 0, :, 0], send_b2.at[k])
+        return 0
+
+    lax.fori_loop(1, n_a, done_first_a, 0)
+    lax.fori_loop(1, n_b, done_first_b, 0)
+    lax.fori_loop(1, n_a2, done_second_a, 0)
+    lax.fori_loop(1, n_b2, done_second_b, 0)
+
+    @pl.when(even)
+    def _():
+        done_second_a(0, 0)
+
+    @pl.when(jnp.logical_not(even))
+    def _():
+        done_second_b(0, 0)
+
     for copy in copies:
         copy.wait_send()
 
@@ -411,16 +591,33 @@
     down_weight,
 ):
     vmem = pl.BlockSpec(memory_space=pltpu.VMEM)
-    perm = jnp.asarray(cell_permutation(), jnp.bfloat16)
     slab = 2 * n_lon
+    n_yl, n_x, n_c, n_yh, n_z = grid_of(n_lon, n_lat)
     out = pl.pallas_call(
         functools.partial(kernel, n_lon, n_lat),
-        out_shape=jax.ShapeDtypeStruct((288, 384), jnp.bfloat16),
-        in_specs=[pl.BlockSpec(memory_space=pl.ANY)] + [vmem] * 14,
+        out_shape=jax.ShapeDtypeStruct((576, 192), jnp.bfloat16),
+        in_specs=[pl.BlockSpec(memory_space=pltpu.HBM)] * 14,
         out_specs=vmem,
         scratch_shapes=[
-            pltpu.VMEM((n_lon, n_lat, 2, 128), jnp.bfloat16),
-            pltpu.VMEM((n_lat, n_lon, 2, 128), jnp.bfloat16),
+            pltpu.VMEM((n_lat, 2, n_lon), jnp.int32),
+            pltpu.VMEM((n_lat, 2, n_lon), jnp.int32),
+            pltpu.VMEM((n_lat, n_lon), jnp.int32),
+            pltpu.VMEM((288, 2, 192), jnp.bfloat16),
+            pltpu.VMEM((192, 128), jnp.bfloat16),
+            pltpu.VMEM((INSTR, 192), jnp.bfloat16),
+            pltpu.VMEM((192, 384), jnp.bfloat16),
+            pltpu.VMEM((192,), jnp.bfloat16),
+            pltpu.VMEM((192, 576), jnp.bfloat16),
+            pltpu.VMEM((192, 192), jnp.bfloat16),
+            pltpu.VMEM((192,), jnp.bfloat16),
+            pltpu.VMEM((192, 768), jnp.bfloat16),
+            pltpu.VMEM((192, 768), jnp.bfloat16),
+            pltpu.VMEM((TOKENS, 576), jnp.bfloat16),
+            pltpu.VMEM((576, TOKENS), jnp.bfloat16),
+            pltpu.SemaphoreType.DMA((13,)),
+            pltpu.VMEM((n_yh, n_yl, n_c, n_x // 2, n_z, 2, 128), jnp.bfloat16),
+            pltpu.VMEM((n_z, n_x, n_yl // 2, n_c, n_yh, 2, 128), jnp.bfloat16),
+            pltpu.VMEM((n_yh, n_z, n_yl, n_x, n_c, 2, 128), jnp.bfloat16),
             pltpu.VMEM((n_lon, 1, 128), jnp.float32),
             pltpu.VMEM((n_lon, 1, 128), jnp.float32),
             pltpu.VMEM((n_lat, 8, 128), jnp.float32),
@@ -428,23 +625,26 @@
             pltpu.VMEM((CELLS, n_lat * slab), jnp.bfloat16),
             pltpu.VMEM((n_lat * slab, 512), jnp.bfloat16),
             pltpu.VMEM((TOKENS, 192), jnp.bfloat16),
-            pltpu.VMEM((TOKENS, 192), jnp.bfloat16),
-            pltpu.VMEM((HALO, 192), jnp.bfloat16),
+            pltpu.VMEM((TOKENS, 256), jnp.bfloat16),
+            pltpu.VMEM((HALO, 256), jnp.bfloat16),
             pltpu.VMEM((TOKENS, 192), jnp.bfloat16),
             pltpu.VMEM((TOKENS, 192), jnp.bfloat16),
             pltpu.VMEM((TOKENS, 192), jnp.bfloat16),
             pltpu.VMEM((HALO, 192), jnp.bfloat16),
             pltpu.VMEM((HALO, 192), jnp.bfloat16),
             pltpu.VMEM((TOKENS, 192), jnp.bfloat16),
-            pltpu.VMEM((CELLS, 384), jnp.float32),
+            pltpu.VMEM((TOKENS, 192), jnp.float32),
             pltpu.SemaphoreType.DMA((2,)),
+            pltpu.SemaphoreType.DMA((n_yh * n_yl * n_c,)),
+            pltpu.SemaphoreType.DMA((n_x * n_z,)),
+            pltpu.SemaphoreType.DMA((n_yh * n_yl * n_c // 2,)),
+            pltpu.SemaphoreType.DMA((n_x * n_z // 2,)),
             pltpu.SemaphoreType.DMA,
             pltpu.SemaphoreType.DMA,
             pltpu.SemaphoreType.DMA,
             pltpu.SemaphoreType.DMA,
             pltpu.SemaphoreType.DMA,
             pltpu.SemaphoreType.DMA,
-            pltpu.SemaphoreType.DMA((n_lat,)),
             pltpu.SemaphoreType.DMA((n_lat,)),
             pltpu.SemaphoreType.DMA((9,)),
             pltpu.SemaphoreType.DMA((9,)),
@@ -453,19 +653,18 @@
             collective_id=0, has_side_effects=True, vmem_limit_bytes=40 * 1024 * 1024
         ),
     )(
-        record_values,
+        record_values.reshape(n_yl // 2, 2, n_x // 2, 2, n_c, n_yh, n_z, 2, 128),
         record_cell.transpose(1, 2, 0),
         record_instrument.transpose(1, 2, 0),
         block_counts.transpose(1, 0),
-        background.reshape(288, 384),
-        perm,
+        background.reshape(288, 2, 192),
         input_weight.T,
         instrument_table,
         lift_weight,
-        first_gain.reshape(1, 192),
+        first_gain,
         attn_weight,
         mix_weight,
-        second_gain.reshape(1, 192),
+        second_gain,
         up_weight,
         down_weight.T,
     )

time: 91.3 us -> 90.4 us (level)
  the two profiles are of different devices: /device:TPU:3 before, /device:TPU:1 now
where the time goes in v2:
time: 90.4 us; the launch traced here: 89.8 us
  Pallas kernels  79.3 us (88%)
  local copies, waits for them, and re-layouts  10.5 us (12%)
    pallas_call x1, Pallas kernels, local(): pl.pallas_call(functools.partial(kernel, n_lon, n_lat), out_shape=jax.Sha...  79.3 us
    unnamed x28, local copies, waits for them, and re-layouts  9.6 us

profile of v2, /device:TPU:1, one launch (start us, length us, event | category | flops | bytes accessed | tf_op | source)
XLA Modules:
  0.0 89.8 jit_solution(2901128443058795284)
XLA Ops:
  0.0 0.0 copy-start.10
  0.0 0.0 copy-start.11
  0.0 0.0 copy-start.12
  0.0 0.0 copy-start.13
  0.0 0.7 copy-done.10
  0.7 0.0 copy-done.11
  0.7 0.0 copy-done.12
  0.7 0.0 copy-done.13
  0.7 0.0 copy-start
  0.7 1.0 %copy-done = bf16[64,16,2,128]{3,2,1,0:T(2,128)(2,1)S(1)} copy-done((bf16[64,16,2,128]{3,2,1,0:T(2,128)(2,1)S(1)}, bf16[64,16,2,128]{3,2,1,0:T(2,128)(2,1)}, u32[]{:S(2)}) %copy-start) | copy-done | bytes 524312
  1.8 0.0 copy-start.1
  1.8 1.0 %copy-done.1 = bf16[12,24,2,192]{3,2,1,0:T(2,128)(2,1)S(1)} copy-done((bf16[12,24,2,192]{3,2,1,0:T(2,128)(2,1)S(1)}, bf16[12,24,2,192]{3,2,1,0:T(2,128)(2,1)}, u32[]{:S(2)}) %copy-start.1) | copy-done | bytes 221208
  2.7 0.0 copy-start.2
  2.7 1.0 %copy-done.2 = bf16[192,768]{1,0:T(8,128)(2,1)S(1)} copy-done((bf16[192,768]{1,0:T(8,128)(2,1)S(1)}, bf16[192,768]{1,0:T(8,128)(2,1)}, u32[]{:S(2)}) %copy-start.2) | copy-done | bytes 294936
  3.7 0.0 copy-start.3
  3.7 1.0 %copy-done.3 = bf16[768,192]{0,1:T(8,128)(2,1)S(1)} copy-done((bf16[768,192]{0,1:T(8,128)(2,1)S(1)}, bf16[768,192]{0,1:T(8,128)(2,1)}, u32[]{:S(2)}) %copy-start.3) | copy-done | bytes 294936
  4.6 0.0 copy-start.4
  4.6 0.9 %copy-done.4 = bf16[192,576]{1,0:T(8,128)(2,1)S(1)} copy-done((bf16[192,576]{1,0:T(8,128)(2,1)S(1)}, bf16[192,576]{1,0:T(8,128)(2,1)}, u32[]{:S(2)}) %copy-start.4) | copy-done | bytes 221208
  5.6 0.0 copy-start.5
  5.6 0.9 %copy-done.5 = bf16[192,384]{1,0:T(8,128)(2,1)S(1)} copy-done((bf16[192,384]{1,0:T(8,128)(2,1)S(1)}, bf16[192,384]{1,0:T(8,128)(2,1)}, u32[]{:S(2)}) %copy-start.5) | copy-done | bytes 147480
  6.5 0.0 copy-start.6
  6.5 0.9 copy-done.6
  7.4 0.0 copy-start.7
  7.4 0.8 copy-done.7
  8.2 0.0 copy-start.8
  8.2 0.7 copy-done.8
  8.9 0.0 copy-start.9
  8.9 0.7 copy-done.9
  9.6 79.3 %shard_map.136 = bf16[576,192]{1,0:T(8,128)(2,1)S(1)} custom-call(bf16[2,2,4,2,2,2,8,2,128]{8,7,6,5,4,3,2,1,0:T(2,128)(2,1)S(1)} %bitcast.7, s32[16,2,64]{2,1,0:T(2,128)S(1)} %bitcast.11, s32[16,2,64]{2,1,0:T(2,128)S(1)} %bitcast.12, s32[16,64]{1,0:T(8,128)S(1)} %bitcast.13, bf16[288,2,192]{2,1,0:T(2,128)(2,1)S(1)} %bitcast.8, ...), custom_call_target="tpu_custom_call" | custom-call | tf_op jit(solution)/shard_map/pallas_call | solution.py:596
  89.0 0.9 reshape.11
Async XLA Ops:
  0.0 0.7 copy-start.10
  0.0 0.7 copy-start.11
  0.0 0.7 copy-start.12
  0.0 0.7 copy-start.13
  0.7 1.0 %copy-start = (bf16[64,16,2,128]{3,2,1,0:T(2,128)(2,1)S(1)}, bf16[64,16,2,128]{3,2,1,0:T(2,128)(2,1)}, u32[]{:S(2)}) copy-start(bf16[64,16,2,128]{3,2,1,0:T(2,128)(2,1)} %param.14) | copy-start | bytes 1572868
  1.8 1.0 %copy-start.1 = (bf16[12,24,2,192]{3,2,1,0:T(2,128)(2,1)S(1)}, bf16[12,24,2,192]{3,2,1,0:T(2,128)(2,1)}, u32[]{:S(2)}) copy-start(bf16[12,24,2,192]{3,2,1,0:T(2,128)(2,1)} %param.18) | copy-start | bytes 663556
  2.7 1.0 %copy-start.2 = (bf16[192,768]{1,0:T(8,128)(2,1)S(1)}, bf16[192,768]{1,0:T(8,128)(2,1)}, u32[]{:S(2)}) copy-start(bf16[192,768]{1,0:T(8,128)(2,1)} %up_hbm.1) | copy-start | bytes 884740
  3.7 1.0 %copy-start.3 = (bf16[768,192]{0,1:T(8,128)(2,1)S(1)}, bf16[768,192]{0,1:T(8,128)(2,1)}, u32[]{:S(2)}) copy-start(bf16[768,192]{0,1:T(8,128)(2,1)} %param.27) | copy-start | bytes 884740
  4.6 0.9 %copy-start.4 = (bf16[192,576]{1,0:T(8,128)(2,1)S(1)}, bf16[192,576]{1,0:T(8,128)(2,1)}, u32[]{:S(2)}) copy-start(bf16[192,576]{1,0:T(8,128)(2,1)} %attn_hbm.1) | copy-start | bytes 663556
  5.6 0.9 %copy-start.5 = (bf16[192,384]{1,0:T(8,128)(2,1)S(1)}, bf16[192,384]{1,0:T(8,128)(2,1)}, u32[]{:S(2)}) copy-start(bf16[192,384]{1,0:T(8,128)(2,1)} %lift_hbm.1) | copy-start | bytes 442372
  6.5 0.9 copy-start.6
  7.4 0.8 copy-start.7
  8.2 0.7 copy-start.8
  8.9 0.7 copy-start.9

commit v3 on v2

--- a/solution.py
+++ b/solution.py
@@ -424,7 +424,7 @@
         lifted_s[pl.ds(at, slab), 0:384] = lifted
         return 0
 
-    lax.fori_loop(0, n_lat, encode, 0)
+    lax.fori_loop(0, n_lat, encode, 0, unroll=2)
 
     total = dot_nn(onehot_s[...], lifted_s[...])
     tally = 1.0 + total[:, 384:385]
@@ -650,7 +650,7 @@
             pltpu.SemaphoreType.DMA((9,)),
         ],
         compiler_params=pltpu.CompilerParams(
-            collective_id=0, has_side_effects=True, vmem_limit_bytes=40 * 1024 * 1024
+            collective_id=0, has_side_effects=True, vmem_limit_bytes=60 * 1024 * 1024
         ),
     )(
         record_values.reshape(n_yl // 2, 2, n_x // 2, 2, n_c, n_yh, n_z, 2, 128),

time: 90.4 us -> 79.4 us (0.88)
  local copies, waits for them, and re-layouts: 10.5 us -> 1.83 us
  Pallas kernels: 79.3 us -> 77.4 us
    unnamed x28 -> x0, local copies, waits for them, and re-layouts: 9.6 us -> none
    pallas_call x1, Pallas kernels: 79.3 us -> 77.4 us  [local(): pl.pallas_call(functools.partial(kernel, n_lon, n_lat), out_shape=jax.Sha...]
    reshape x1, local copies, waits for them, and re-layouts: 0.86 us -> 1.83 us  [local(): return out.reshape(12, 24, 2, 192)]
where the time goes in v3:
time: 79.4 us; the launch traced here: 79.2 us
  Pallas kernels  77.4 us (97%)
  local copies, waits for them, and re-layouts  1.83 us (2%)
    pallas_call x1, Pallas kernels, local(): pl.pallas_call(functools.partial(kernel, n_lon, n_lat), out_shape=jax.Sha...  77.4 us
    reshape x1, local copies, waits for them, and re-layouts, local(): return out.reshape(12, 24, 2, 192)  1.83 us

profile of v3, /device:TPU:1, one launch (start us, length us, event | category | flops | bytes accessed | tf_op | source)
XLA Modules:
  0.0 79.2 jit_solution(17992322259126662216)
XLA Ops:
  0.0 77.4 %shard_map.136 = bf16[576,192]{1,0:T(8,128)(2,1)} custom-call(bf16[2,2,4,2,2,2,8,2,128]{8,7,6,5,4,3,2,1,0:T(2,128)(2,1)} %bitcast.7, s32[16,2,64]{2,1,0:T(2,128)} %bitcast.11, s32[16,2,64]{2,1,0:T(2,128)} %bitcast.12, s32[16,64]{1,0:T(8,128)} %bitcast.13, bf16[288,2,192]{2,1,0:T(2,128)(2,1)} %bitcast.8, bf16[192,128]{1,0:T(8,128)(2,1)} %bitcast.10, ...), custom_call_target="tpu_custom_call" | custom-call | tf_op jit(solution)/shard_map/pallas_call | solution.py:596
  77.4 1.8 %reshape.11 = bf16[12,24,2,192]{3,2,1,0:T(2,128)(2,1)} reshape(bf16[576,192]{1,0:T(8,128)(2,1)} %shard_map.136) | data formatting | bytes 442368 | tf_op jit(solution)/shard_map/reshape | solution.py:671
